TPU v7x, 512 devices: a whole 4x4x16 slice. The times are simulated.
512 devices in a mesh: section: 16 (over x, z_lo), dp: 32 (over z_hi, y, core).
Axes of the slice: x: 4, y: 4, z: 16 (z_hi: 4, z_lo: 4; z = z_hi * 4 + z_lo), core: 2. Of those that a mesh axis runs over, the one named last changes fastest.
Arguments:
- activations: bfloat16 [16, 4096, 8192], P('section', 'dp'), may hold values from -6 to 6
- out_grads: bfloat16 [16, 4096, 1024], P('section', 'dp'), may hold values from -1.5 to 1.5
- in_basis: bfloat16 [16, 8192, 256], P('section', 'dp'), may hold values from -0.375 to 0.375
- out_basis: bfloat16 [16, 1024, 1024], P('section', 'dp'), may hold values from -0.1875 to 0.1875
- curvature: bfloat16 [16, 1024, 8192], P('section', None, 'dp'), may hold values from 2 to 32
- left_factors: bfloat16 [16, 32, 32, 1024], P('section', 'dp'), may hold values from -0.1875 to 0.1875
- right_factors: bfloat16 [16, 32, 32, 8192], P('section', None, None, 'dp'), may hold values from -0.0625 to 0.0625
- sequence_ids: int32 [32], replicated, may hold values from 0 to 31, each once
- query_order: int32 [32], replicated, may hold values from 0 to 31, each once
Outputs:
- influence: float32 [16, 32, 32], P('section', 'dp')
Inputs may be any that keep to these rules, and one draw needn't show every extreme that they name: `sequence_ids`: a permutation: each output row receives exactly one training sequence. `query_order`: a permutation: each query is stored in exactly one slot.
All inputs are finite; a program needn't handle non-finite values.
Results may differ from a plain program's by a relative error of at most 0.0057.
Values may be sent and summed in bfloat16 or wider, within the bound.
A program may use at most 128 MiB of HBM per device.

v0:
```python
import math

import jax
import jax.numpy as jnp
from jax import lax
from jax.sharding import PartitionSpec as P

SEQ_LEN = 128


def carried_in(part, axis, combine, identity):
    count = lax.axis_size(axis)
    place = lax.axis_index(axis)
    ahead = count - 1 - place
    gathered = lax.all_gather(part, axis)
    state = jnp.zeros_like(part) + jnp.asarray(identity, part.dtype)

    def one(lap, state):
        source = count - 1 - lap
        return combine(state, lax.dynamic_index_in_dim(gathered, source, 0, False))

    return lax.fori_loop(0, ahead, one, state)


def add_scores(earlier, later):
    return earlier + later


def on_device(
    activations,
    out_grads,
    in_basis,
    out_basis,
    curvature,
    left_factors,
    right_factors,
    sequence_ids,
    query_order,
):
    layer_acts = activations[0]
    layer_grads = out_grads[0]
    block_basis = in_basis[0]
    columns = block_basis.shape[0]
    block_size = block_basis.shape[1]
    n_blocks = columns // block_size
    grouped_basis = block_basis.reshape(n_blocks, block_size, block_size)
    basis_rows, left_all = (
        lax.all_gather(out_basis[0], "dp", axis=0, tiled=True),
        lax.all_gather(left_factors[0], "dp", axis=0, tiled=True),
    )
    rotated_own = jnp.dot(layer_grads, basis_rows, preferred_element_type=jnp.float32).astype(
        jnp.bfloat16
    )
    all_signals = lax.all_gather(rotated_own, "dp", axis=0, tiled=True)
    feature_cols = lax.all_to_all(layer_acts, "dp", split_axis=1, concat_axis=0, tiled=True)
    token_count = feature_cols.shape[0]
    grouped_cols = feature_cols.reshape(token_count, n_blocks, block_size)
    rotated_acts = jnp.einsum(
        "tbi,bij->tbj", grouped_cols, grouped_basis, preferred_element_type=jnp.float32
    )
    rotated_acts = rotated_acts.astype(jnp.bfloat16).reshape(token_count, columns)
    seq_count = token_count // SEQ_LEN
    group_size = math.gcd(seq_count, 8)
    out_width = all_signals.shape[1]
    signal_groups = all_signals.reshape(seq_count // group_size, group_size, SEQ_LEN, out_width)
    act_groups = rotated_acts.reshape(seq_count // group_size, group_size, SEQ_LEN, columns)
    divisor = curvature[0].astype(jnp.float32)

    def rescale(operands):
        gradient = jnp.einsum(
            "nti,ntj->nij", operands[0], operands[1], preferred_element_type=jnp.float32
        )
        return (gradient / divisor).astype(jnp.bfloat16)

    scaled = lax.map(rescale, (signal_groups, act_groups)).reshape(seq_count, out_width * columns)
    right_all = right_factors[0]
    query_count = right_all.shape[0]
    rank_size = right_all.shape[1]
    query_group = math.gcd(query_count, 8)

    def expand(operands):
        product = jnp.einsum(
            "qri,qrj->qij", operands[0], operands[1], preferred_element_type=jnp.float32
        )
        return product.astype(jnp.bfloat16)

    query_mats = lax.map(
        expand,
        (
            left_all.reshape(query_count // query_group, query_group, rank_size, out_width),
            right_all.reshape(query_count // query_group, query_group, rank_size, columns),
        ),
    )
    query_mats = query_mats.reshape(query_count, out_width * columns)
    scores = lax.dot_general(
        scaled, query_mats, (((1,), (1,)), ((), ())), preferred_element_type=jnp.float32
    )
    row_pick = (sequence_ids[None, :] == jnp.arange(seq_count, dtype=jnp.int32)[:, None]).astype(
        jnp.float32
    )
    col_pick = (query_order[:, None] == jnp.arange(query_count, dtype=jnp.int32)[None, :]).astype(
        jnp.float32
    )
    placed = jnp.dot(
        jnp.dot(row_pick, scores, precision=lax.Precision.HIGHEST),
        col_pick,
        precision=lax.Precision.HIGHEST,
    )
    layer_part = lax.psum_scatter(placed, "dp", scatter_dimension=0, tiled=True)
    deeper = carried_in(layer_part, "section", add_scores, jnp.zeros_like(layer_part))
    total = deeper + layer_part
    return total[None]


def solution(mesh):
    placed = (
        P("section", "dp", None),
        P("section", "dp", None),
        P("section", "dp", None),
        P("section", "dp", None),
        P("section", None, "dp"),
        P("section", "dp", None, None),
        P("section", None, None, "dp"),
        P(),
        P(),
    )
    return jax.shard_map(
        on_device, mesh=mesh, in_specs=placed, out_specs=P("section", "dp", None), check_vma=False
    )
```

profile of v0, /device:TPU:32, one launch (start us, length us, event | category | flops | bytes accessed | tf_op | source)
XLA Modules:
  0.0 662.1 jit_solution(11100165442802626134)
XLA Ops:
  6.5 0.7 all-gather.10.cloned.1.call-update
  7.3 0.7 all-gather.12.cloned.1.call-update
  8.1 81.7 %all-gather.10.cloned.1.call-done = bf16[1,1024,1024]{2,1,0:T(8,128)(2,1)} async-done(((bf16[1,32,1024]{2,1,0:T(8,128)(2,1)}), bf16[1,1024,1024]{2,1,0:T(8,128)(2,1)}) %all-gather.10.cloned.1.call-update) | async-done | bytes 2097168 | tf_op jit(solution)/shard_map/all_gather | solution.py:48
  89.8 2.7 fusion.13
  92.5 4.1 copy.18
  96.7 9.2 %all-to-all-start = ((bf16[128,32,256]{0,2,1:T(8,128)(2,1)}), bf16[128,32,256]{0,2,1:T(8,128)(2,1)S(1)}, u32[]{:S(2)}, u32[]{:S(2)}) async-start(bf16[128,32,256]{0,2,1:T(8,128)(2,1)} %bitcast.77), calls=%async_computation | async-start | bytes 4194304 | tf_op jit(solution)/shard_map/all_to_all | solution.py:55
  105.8 1.3 dynamic-slice
  107.2 1.1 bitcast_convert_fusion
  108.3 142.7 %all-gather.12.cloned.1.call-done = bf16[32,1,32,1024]{3,2,1,0:T(8,128)(2,1)} async-done(((bf16[1,1,32,1024]{3,2,1,0:T(8,128)(2,1)}), bf16[32,1,32,1024]{3,2,1,0:T(8,128)(2,1)}) %all-gather.12.cloned.1.call-update) | async-done | bytes 2097168 | tf_op jit(solution)/shard_map/all_gather | solution.py:49
  251.0 5.9 broadcast.6.clone.1
  256.9 17.3 %while.33 = (s32[]{:T(128)}, bf16[4,8,1024,256]{3,2,1,0:T(8,128)(2,1)}, bf16[4,8,32,1024]{3,2,1,0:T(8,128)(2,1)}, bf16[4,8,32,256]{3,2,1,0:T(8,128)(2,1)}, s32[]{:T(128)}) while((s32[]{:T(128)}, bf16[4,8,1024,256]{3,2,1,0:T(8,128)(2,1)}, bf16[4,8,32,1024]{3,2,1,0:T(8,128)(2,1)}, bf16[4,8,32,256]{3,2,1,0:T(8,128)(2,1)}, s32[]{:T(128)}) %tuple.73), condition=%wide.region_3.4_spmd, body=%wide.region_2.3_spmd.sunk | while | flops 136314880 | bytes 4851261 | solution.py:87
  256.9 4.3 bitcast_dynamic-update-slice_fusion.5
  261.2 4.3 bitcast_dynamic-update-slice_fusion.5
  265.6 4.3 bitcast_dynamic-update-slice_fusion.5
  269.9 4.3 bitcast_dynamic-update-slice_fusion.5
  274.2 17.9 %copy.25 = bf16[4,8,1024,256]{3,1,2,0:T(8,128)(2,1)} copy(bf16[4,8,1024,256]{3,2,1,0:T(8,128)(2,1)} %get-tuple-element.111) | data formatting | bytes 33554432
  292.2 2.9 copy.19
  295.1 2.4 fusion.10
  297.4 2.5 copy.22
  299.9 64.4 %all-gather.8.cloned.1.call-done = bf16[4096,1024]{1,0:T(8,128)(2,1)} async-done(((bf16[128,1024]{1,0:T(8,128)(2,1)}), bf16[4096,1024]{1,0:T(8,128)(2,1)}) %all-gather.8.cloned.1.call-update) | async-done | bytes 8388624 | tf_op jit(solution)/shard_map/all_gather | solution.py:54
  364.4 5.9 broadcast.6.clone
  370.2 19.8 %while.32 = (s32[]{:T(128)}, bf16[4,8,1024,256]{3,2,1,0:T(8,128)(2,1)}, bf16[4,8,128,1024]{3,2,1,0:T(8,128)(2,1)}, bf16[4,8,128,256]{3,2,1,0:T(8,128)(2,1)}, f32[1024,256]{1,0:T(8,128)S(1)}, /*index=5*/s32[]{:T(128)}) while((s32[]{:T(128)}, bf16[4,8,1024,256]{3,2,1,0:T(8,128)(2,1)}, bf16[4,8,128,1024]{3,2,1,0:T(8,128)(2,1)}, ...), condition=%wide.region_1.2_spmd, body=%wide.region_0.1_spmd.sunk | while | flops 541065216 | bytes 7865925 | solution.py:75
  370.2 4.9 bitcast_dynamic-update-slice_fusion.4
  375.2 5.0 bitcast_dynamic-update-slice_fusion.4
  380.1 4.9 bitcast_dynamic-update-slice_fusion.4
  385.1 4.9 bitcast_dynamic-update-slice_fusion.4
  390.0 17.9 %copy.24 = bf16[4,8,1024,256]{3,1,2,0:T(8,128)(2,1)} copy(bf16[4,8,1024,256]{3,2,1,0:T(8,128)(2,1)} %get-tuple-element.110) | data formatting | bytes 33554432
  407.9 12.9 %fusion.23 = f32[32,32]{1,0:T(8,128)S(1)} fusion(bf16[32,262144]{1,0:T(8,128)(2,1)} %bitcast.75, bf16[32,262144]{1,0:T(8,128)(2,1)} %bitcast.74), kind=kOutput, calls=%fused_computation.31 | convolution fusion | flops 536870912 | bytes 33558528 | tf_op jit(solution)/shard_map/dot_general | solution.py:95
  421.1 168.4 %all-reduce = f32[32,32]{1,0:T(8,128)S(1)} all-reduce(f32[32,32]{1,0:T(8,128)S(1)} %fusion.19), channel_id=5, replica_groups=mesh['section'=16,'dp'=32] {'dp'}, use_global_device_ids=true, to_apply=%region_4.5.clone | all-reduce | flops 1024 | bytes 8192
  589.5 0.6 fusion.22
  590.2 63.7 %all-gather.3 = f32[16,1,32]{2,1,0:T(1,128)S(1)} all-gather(f32[1,1,32]{2,1,0:T(1,128)S(1)} %fusion.22), channel_id=4, replica_groups=mesh['section'=16,'dp'=32] {'section'}, dimensions={0}, use_global_device_ids=true | all-gather | bytes 2176 | tf_op jit(solution)/shard_map/all_gather | solution.py:15
  654.4 1.1 add_bitcast_fusion
  (33 shorter events, 1.1 us)
Async XLA Ops:
  6.5 83.2 %copy-start = (bf16[1,128,1024]{2,1,0:T(8,128)(2,1)S(1)}, bf16[1,128,1024]{2,1,0:T(8,128)(2,1)}, u32[]{:S(2)}) copy-start(bf16[1,128,1024]{2,1,0:T(8,128)(2,1)} %param.16) | copy-start | bytes 786436
  6.5 83.2 %all-gather.10.cloned.1.call-start = ((), (), s32[]{:S(2)}) async-start(), calls=%async_computation.2 | async-start | bytes 2162688 | tf_op jit(solution)/shard_map/all_gather | solution.py:48
  7.3 243.8 %all-gather.12.cloned.1.call-start = ((), (), s32[]{:S(2)}) async-start(), calls=%async_computation.3 | async-start | bytes 2162688 | tf_op jit(solution)/shard_map/all_gather | solution.py:49
  8.0 356.3 %all-gather.8.cloned.1.call-start = ((), (), s32[]{:S(2)}) async-start(), calls=%async_computation.1 | async-start | bytes 8650752 | tf_op jit(solution)/shard_map/all_gather | solution.py:54
  96.7 195.5 %all-to-all-start = ((bf16[128,32,256]{0,2,1:T(8,128)(2,1)}), bf16[128,32,256]{0,2,1:T(8,128)(2,1)S(1)}, u32[]{:S(2)}, u32[]{:S(2)}) async-start(bf16[128,32,256]{0,2,1:T(8,128)(2,1)} %bitcast.77), calls=%async_computation | async-start | bytes 4194304 | tf_op jit(solution)/shard_map/all_to_all | solution.py:55
  274.2 20.8 %copy-start.2 = (bf16[1,256,256]{2,1,0:T(8,128)(2,1)S(1)}, bf16[1,256,256]{2,1,0:T(8,128)(2,1)}, u32[]{:S(2)}) copy-start(bf16[1,256,256]{2,1,0:T(8,128)(2,1)} %param.17) | copy-start | bytes 393220
  407.9 12.9 %copy-start.3 = (s32[32]{0:T(128)S(1)}, s32[32]{0:T(128)}, u32[]{:S(2)}) copy-start(s32[32]{0:T(128)} %param.22) | copy-start | bytes 388
  407.9 13.0 %copy-start.4 = (s32[32]{0:T(128)S(1)}, s32[32]{0:T(128)}, u32[]{:S(2)}) copy-start(s32[32]{0:T(128)} %param.23) | copy-start | bytes 388
  407.9 247.7 %copy-start.1 = (bf16[1,128,1024]{2,1,0:T(8,128)(2,1)S(1)}, bf16[1,128,1024]{2,1,0:T(8,128)(2,1)}, u32[]{:S(2)}) copy-start(bf16[1,128,1024]{2,1,0:T(8,128)(2,1)} %param.16) | copy-start | bytes 786436
Sparse Core Ops, SparseCore 0:
  10.5 79.2 all-gather.9
  92.9 158.0 all-gather.11
  254.2 110.1 all-gather.7
where the time goes:
time: 663 us; the launch traced here: 662 us
  waiting for transfers between devices  290 us (44%)
  blocking collectives  232 us (35%)
  local copies, waits for them, and re-layouts  59 us (9%)
  matrix products  55.4 us (8%)
  between operations  13.2 us (2%)
  starting transfers between devices  9.25 us (1%)
    unnamed x1, blocking collectives  168 us
    all_gather x1, waiting for transfers between devices, on_device(): lax.all_gather(left_factors[0], 'dp', axis=0, tiled=True)  143 us
    all_gather x1, waiting for transfers between devices, on_device(): lax.all_gather(out_basis[0], 'dp', axis=0, tiled=True)  81.7 us
    all_gather x1, waiting for transfers between devices, on_device(): all_signals = lax.all_gather(rotated_own, 'dp', axis=0, tiled=True)  64.4 us
    all_gather x1, blocking collectives, carried_in(): gathered = lax.all_gather(part, axis)  63.7 us
    unnamed x15, local copies, waits for them, and re-layouts  41.9 us
    dot_general x4, matrix products, rescale(): jnp.einsum('nti,ntj->nij', operands[0], operands[1], preferred_element_ty...  19.8 us
    dot_general x4, matrix products, expand(): jnp.einsum('qri,qrj->qij', operands[0], operands[1], preferred_element_ty...  17.3 us
  transfers between devices with their start and end apart: 4, of which 3 were waited for; matrix products, arithmetic and copies ran while one was open for 9% of the time, Pallas kernels for 0%

commit v1 on v0

v1 whole, which is shorter than its diff:
```python
import jax
import jax.numpy as jnp
from jax import lax
from jax.experimental import pallas as pl
from jax.experimental.pallas import tpu as pltpu
from jax.sharding import PartitionSpec as P

MESH = pl.DeviceIdType.MESH
F32 = jnp.float32
BF16 = jnp.bfloat16
HI = lax.Precision.HIGHEST


def kernel(
    acts,
    grads,
    in_basis,
    out_basis,
    curv,
    left,
    right,
    seq_ids,
    q_order,
    out,
    small,
    big,
    cols,
    basis_v,
    left_v,
    ub_v,
    curv_v,
    inv_v,
    right_v,
    scaled_v,
    part_v,
    rows_v,
    row_send,
    row_recv,
    sec_send,
    sec_recv,
    small_ss,
    small_rs,
    big_ss,
    big_rs,
    col_ss,
    col_rs,
    row_ss,
    row_rs,
    sec_ss,
    sec_rs,
    loc,
):
    n_dev = 32
    n_sec = 16
    me = lax.axis_index("dp")
    sec = lax.axis_index("section")
    z = me // 8
    sub = me % 8
    y = sub // 2
    c = sub % 2
    step = 1 - 2 * c
    width = cols.shape[2]

    def slot(dz, dy, core):
        return ((z + dz + 8) % 4) * 8 + ((y + dy + 8) % 4) * 2 + core

    partner = slot(0, 0, 1 - c)

    own_cols = pl.ds(pl.multiple_of(me * width, width), width)
    l_u = pltpu.make_async_copy(out_basis, small.at[me, pl.ds(0, 32)], loc.at[0])
    l_l = pltpu.make_async_copy(left, small.at[me, pl.ds(32, 32)], loc.at[1])
    l_g = pltpu.make_async_copy(grads, big.at[me], loc.at[2])
    l_c = pltpu.make_async_copy(curv, curv_v, loc.at[3])
    l_r = pltpu.make_async_copy(right, right_v, loc.at[4])
    l_b = pltpu.make_async_copy(in_basis, ub_v, loc.at[5])
    l_a = pltpu.make_async_copy(acts.at[:, own_cols], cols.at[me], col_rs.at[me])
    for cp in (l_u, l_l, l_g, l_a, l_c, l_r, l_b):
        cp.start()

    barrier = pltpu.get_barrier_semaphore()

    def greet(o, _):
        pl.semaphore_signal(
            barrier, inc=1, device_id={"dp": (me + o) % n_dev}, device_id_type=MESH
        )
        return 0

    def greet_sec(o, _):
        pl.semaphore_signal(
            barrier, inc=1, device_id={"section": (sec + o) % n_sec}, device_id_type=MESH
        )
        return 0

    lax.fori_loop(1, n_dev, greet, 0)
    lax.fori_loop(1, n_sec, greet_sec, 0)
    rows_v[...] = jnp.zeros_like(rows_v)
    l_u.wait()
    l_l.wait()
    l_g.wait()
    pl.semaphore_wait(barrier, n_dev - 1 + n_sec - 1)

    counts = {"small": 0, "big": 0}
    parts = {"small": (small, small_ss, small_rs), "big": (big, big_ss, big_rs)}

    def copy_of(kind, which, s, dev):
        buf, ss, rs = parts[kind]
        return pltpu.make_async_remote_copy(
            src_ref=buf.at[s],
            dst_ref=buf.at[s],
            send_sem=ss.at[which],
            recv_sem=rs.at[s],
            device_id={"dp": dev},
            device_id_type=MESH,
        )

    def send(kind, s, dev):
        copy_of(kind, counts[kind], s, dev).start()
        counts[kind] += 1

    def landed(kind, s):
        copy_of(kind, 0, s, partner).wait_recv()

    steps = (0, -step, step, 2)

    def z_own(kind):
        send(kind, me, slot(1, 0, c))
        send(kind, me, slot(-1, 0, c))

    def spread(kind, g):
        s = slot(steps[g], 0, c)
        if g > 0:
            landed(kind, s)
        if g == 1:
            send(kind, s, slot(step, 0, c))
        send(kind, s, slot(0, 1, c))
        send(kind, s, slot(0, -1, c))
        send(kind, s, partner)

    def relay(kind, g):
        s = slot(steps[g], -step, c)
        landed(kind, s)
        send(kind, s, slot(0, step, c))
        send(kind, s, partner)
        s = slot(steps[g], step, c)
        landed(kind, s)
        send(kind, s, partner)

    def far(kind, g):
        s = slot(steps[g], 2, c)
        landed(kind, s)
        send(kind, s, partner)

    def other(kind, g):
        for dy in range(4):
            landed(kind, slot(steps[g], dy, 1 - c))

    def col_copy(dst, src_slot):
        return pltpu.make_async_remote_copy(
            src_ref=acts.at[:, pl.ds(pl.multiple_of(dst * width, width), width)],
            dst_ref=cols.at[src_slot],
            send_sem=col_ss.at[dst],
            recv_sem=col_rs.at[src_slot],
            device_id={"dp": dst},
            device_id_type=MESH,
        )

    def col_sends(dzs, lo, hi):
        def one(j, _):
            for dz in dzs:
                dst = ((z + dz + 8) % 4) * 8 + (sub + j) % 8
                col_copy(dst, me).start()
            return 0

        lax.fori_loop(lo, hi, one, 0)

    z_own("small")
    spread("small", 0)
    col_sends((1, -1), 0, 2)
    relay("small", 0)
    spread("small", 1)
    spread("small", 2)
    z_own("big")
    col_sends((1, -1), 2, 8)
    far("small", 0)
    relay("small", 1)
    relay("small", 2)
    spread("big", 0)
    col_sends((0,), 1, 8)
    l_c.wait()
    inv_v[...] = 1.0 / curv_v[...].astype(F32)
    l_r.wait()
    l_b.wait()
    far("small", 1)
    far("small", 2)
    relay("big", 0)
    spread("small", 3)
    relay("small", 3)
    far("big", 0)
    far("small", 3)
    for g in range(4):
        other("small", g)

    def lay(k, _):
        at = pl.ds(pl.multiple_of(k * 32, 32), 32)
        basis_v[at, :] = small[k, 0:32, :]
        left_v[at, :] = small[k, 32:64, :]
        return 0

    lax.fori_loop(0, n_dev, lay, 0)
    other("big", 0)

    ones = jnp.ones((8, 128), F32)

    def sequence(t, _):
        @pl.when(t == 4)
        def _():
            spread("big", 1)
            spread("big", 2)
            col_sends((2,), 0, 8)

        @pl.when(t == 8)
        def _():
            relay("big", 1)
            relay("big", 2)
            far("big", 1)
            far("big", 2)
            other("big", 1)
            other("big", 2)

        @pl.when(t == 20)
        def _():
            spread("big", 3)

        @pl.when(t == 22)
        def _():
            relay("big", 3)

        @pl.when(t == 24)
        def _():
            far("big", 3)
            other("big", 3)

        g = t // 8
        turn = ((g + 3) // 4) * (1 + (g + 1) % 3)
        zz = (z + step * turn + 16) % 4
        n = zz * 8 + (sub - t % 8 + 8) % 8
        col_copy(partner, n).wait_recv()
        acts_n = jnp.dot(cols[n], ub_v[...], preferred_element_type=F32).astype(BF16)
        for i in range(4):
            at = slice(i * 256, (i + 1) * 256)
            grads_n = jnp.dot(big[n], basis_v[:, at], preferred_element_type=F32).astype(BF16)
            gradient = lax.dot_general(
                grads_n, acts_n, (((0,), (0,)), ((), ())), preferred_element_type=F32
            )
            scaled_v[at, :] = (gradient * inv_v[at, :]).astype(BF16)
        for i in range(4):
            at = slice(i * 256, (i + 1) * 256)
            prod = jnp.dot(left_v[at, :], scaled_v[...], preferred_element_type=F32)
            prod = prod.reshape(8, 32, width) * right_v[i * 8 : (i + 1) * 8].astype(F32)
            summed = jnp.sum(prod, axis=1)
            part_v[i * 8 : (i + 1) * 8, :] = summed[:, :128] + summed[:, 128:]
        row = lax.dot_general(
            ones, part_v[...], (((1,), (1,)), ((), ())), precision=HI, preferred_element_type=F32
        )
        rows_v[pl.ds(n, 1), 0:32] = row[0:1]
        return 0

    lax.fori_loop(0, n_dev, sequence, 0)

    row_pick = (seq_ids[...] == lax.broadcasted_iota(jnp.int32, (32, 32), 0)).astype(F32)
    col_pick = (q_order[...] == lax.broadcasted_iota(jnp.int32, (32, 32), 0)).astype(F32)
    placed = jnp.dot(row_pick, rows_v[:, 0:32], precision=HI, preferred_element_type=F32)
    placed = lax.dot_general(
        placed, col_pick, (((1,), (1,)), ((), ())), precision=HI, preferred_element_type=F32
    )
    placed = jnp.concatenate([placed, jnp.zeros((32, 96), F32)], axis=1)
    for m in range(n_dev):
        row_send[m] = placed[m : m + 1]

    if counts != {"small": 31, "big": 31}:
        raise ValueError(str(counts))

    for kind in ("small", "big"):
        for i in range(counts[kind]):
            copy_of(kind, i, me, partner).wait_send()

    def col_left(o, _):
        col_copy((me + o) % n_dev, me).wait_send()
        return 0

    lax.fori_loop(1, n_dev, col_left, 0)

    def row_copy(dst, src_slot):
        return pltpu.make_async_remote_copy(
            src_ref=row_send.at[dst],
            dst_ref=row_recv.at[src_slot],
            send_sem=row_ss.at[dst],
            recv_sem=row_rs.at[src_slot],
            device_id={"dp": dst},
            device_id_type=MESH,
        )

    def row_start(o, _):
        row_copy((me + 15 + o) % n_dev, me).start()
        return 0

    lax.fori_loop(0, 17, row_start, 0)
    lax.fori_loop(18, n_dev, row_start, 0)
    row_recv[me] = row_send[me]

    def row_wait(o, _):
        row_copy(partner, (me + o) % n_dev).wait_recv()
        return 0

    lax.fori_loop(1, n_dev, row_wait, 0)
    total = jnp.sum(row_recv[...], axis=0)
    sec_send[...] = total

    def sec_copy(dst, src_slot):
        return pltpu.make_async_remote_copy(
            src_ref=sec_send,
            dst_ref=sec_recv.at[src_slot],
            send_sem=sec_ss.at[dst],
            recv_sem=sec_rs.at[src_slot],
            device_id={"section": dst},
            device_id_type=MESH,
        )

    def sec_start(o, _):
        sec_copy((sec + o) % n_sec, sec).start()
        return 0

    lax.fori_loop(1, n_sec, sec_start, 0)
    sec_recv[sec] = total

    def row_left(o, _):
        row_copy((me + o) % n_dev, me).wait_send()
        return 0

    lax.fori_loop(1, n_dev, row_left, 0)

    def sec_wait(o, _):
        sec_copy((sec + 1) % n_sec, (sec + o) % n_sec).wait_recv()
        sec_copy((sec + o) % n_sec, sec).wait_send()
        return 0

    lax.fori_loop(1, n_sec, sec_wait, 0)
    layer = lax.broadcasted_iota(jnp.int32, (n_sec, 1, 128), 0)
    kept = jnp.where(layer >= sec, sec_recv[...], 0.0)
    out[...] = jnp.sum(kept, axis=0)[:, 0:32]


def on_device(
    activations,
    out_grads,
    in_basis,
    out_basis,
    curvature,
    left_factors,
    right_factors,
    sequence_ids,
    query_order,
):
    hbm = pl.BlockSpec(memory_space=pl.ANY)
    vmem = pl.BlockSpec(memory_space=pltpu.VMEM)
    sems = pltpu.SemaphoreType.DMA
    total = pl.pallas_call(
        kernel,
        out_shape=jax.ShapeDtypeStruct((1, 32), F32),
        in_specs=[hbm] * 7 + [vmem] * 2,
        out_specs=vmem,
        scratch_shapes=[
            pltpu.VMEM((32, 64, 1024), BF16),
            pltpu.VMEM((32, 128, 1024), BF16),
            pltpu.VMEM((32, 128, 256), BF16),
            pltpu.VMEM((1024, 1024), BF16),
            pltpu.VMEM((1024, 1024), BF16),
            pltpu.VMEM((256, 256), BF16),
            pltpu.VMEM((1024, 256), BF16),
            pltpu.VMEM((1024, 256), F32),
            pltpu.VMEM((32, 32, 256), BF16),
            pltpu.VMEM((1024, 256), BF16),
            pltpu.VMEM((32, 128), F32),
            pltpu.VMEM((32, 128), F32),
            pltpu.VMEM((32, 1, 128), F32),
            pltpu.VMEM((32, 1, 128), F32),
            pltpu.VMEM((1, 128), F32),
            pltpu.VMEM((16, 1, 128), F32),
            sems((31,)),
            sems((32,)),
            sems((31,)),
            sems((32,)),
            sems((32,)),
            sems((32,)),
            sems((32,)),
            sems((32,)),
            sems((16,)),
            sems((16,)),
            sems((6,)),
        ],
        compiler_params=pltpu.CompilerParams(
            collective_id=0, has_side_effects=True, vmem_limit_bytes=56 * 2**20
        ),
        name="influence",
    )(
        activations[0],
        out_grads[0],
        in_basis[0],
        out_basis[0],
        curvature[0],
        left_factors[0, 0],
        right_factors[0],
        sequence_ids[None, :],
        query_order[None, :],
    )
    return total[None]


def solution(mesh):
    placed = (
        P("section", "dp", None),
        P("section", "dp", None),
        P("section", "dp", None),
        P("section", "dp", None),
        P("section", None, "dp"),
        P("section", "dp", None, None),
        P("section", None, None, "dp"),
        P(),
        P(),
    )
    return jax.shard_map(
        on_device, mesh=mesh, in_specs=placed, out_specs=P("section", "dp", None), check_vma=False
    )
```

time: 663 us -> 216 us (0.33)
  the two profiles are of different devices: /device:TPU:32 before, /device:TPU:1 now
where the time goes in v1:
time: 216 us
  Pallas kernels  215 us (100%)
    pallas_call x1, Pallas kernels, on_device(): pl.pallas_call(kernel, out_shape=jax.ShapeDtypeStruct((1, 32), F32), in_s...  215 us

profile of v1, /device:TPU:1, one launch (start us, length us, event | category | flops | bytes accessed | tf_op | source)
XLA Modules:
  0.0 216.0 jit_solution(12919079178988639520)
XLA Ops:
  0.0 214.8 %influence.1 = f32[1,32]{1,0:T(1,128)} custom-call(bf16[128,8192]{1,0:T(8,128)(2,1)} %bitcast.10, bf16[128,1024]{1,0:T(8,128)(2,1)} %bitcast.13, bf16[256,256]{1,0:T(8,128)(2,1)} %bitcast.14, bf16[32,1024]{1,0:T(8,128)(2,1)} %bitcast.15, bf16[1024,256]{1,0:T(8,128)(2,1)} %bitcast.11, bf16[32,1024]{1,0:T(8,128)(2,1)} %bitcast.16, ...), custom_call_target="tpu_custom_call" | custom-call | tf_op jit(solution)/shard_map/influence/pallas_call | solution.py:367
  214.8 1.2 copy.11

commit v2 on v1

--- a/solution.py
+++ b/solution.py
@@ -26,6 +26,7 @@
     big,
     cols,
     basis_v,
+    rotated,
     left_v,
     ub_v,
     curv_v,
@@ -167,7 +168,7 @@
     def col_sends(dzs, lo, hi):
         def one(j, _):
             for dz in dzs:
-                dst = ((z + dz + 8) % 4) * 8 + (sub + j) % 8
+                dst = slot(dz, j // 2, (c + j) % 2)
                 col_copy(dst, me).start()
             return 0
 
@@ -177,14 +178,14 @@
     spread("small", 0)
     col_sends((1, -1), 0, 2)
     relay("small", 0)
+    spread("big", 0)
     spread("small", 1)
     spread("small", 2)
     z_own("big")
-    col_sends((1, -1), 2, 8)
+    col_sends((1, -1), 2, 4)
     far("small", 0)
     relay("small", 1)
     relay("small", 2)
-    spread("big", 0)
     col_sends((0,), 1, 8)
     l_c.wait()
     inv_v[...] = 1.0 / curv_v[...].astype(F32)
@@ -192,9 +193,9 @@
     l_b.wait()
     far("small", 1)
     far("small", 2)
-    relay("big", 0)
     spread("small", 3)
     relay("small", 3)
+    relay("big", 0)
     far("big", 0)
     far("small", 3)
     for g in range(4):
@@ -211,46 +212,72 @@
 
     ones = jnp.ones((8, 128), F32)
 
+    def turn_of(g):
+        return ((g + 3) // 4) * (1 + (g + 1) % 3)
+
+    def rotate(g, _):
+        at = pl.ds(pl.multiple_of(slot(step * turn_of(g), 0, 0) // 8 * 8, 8), 8)
+
+        def chunk(i, _):
+            to = pl.ds(pl.multiple_of(i * 256, 256), 256)
+            turned = jnp.dot(
+                big[at].reshape(1024, 1024), basis_v[:, to], preferred_element_type=F32
+            )
+            rotated[at, :, to] = turned.astype(BF16).reshape(8, 128, 256)
+            return 0
+
+        lax.fori_loop(0, 4, chunk, 0)
+        return 0
+
     def sequence(t, _):
-        @pl.when(t == 4)
+        @pl.when(t == 3)
         def _():
             spread("big", 1)
             spread("big", 2)
+            col_sends((1, -1), 4, 8)
             col_sends((2,), 0, 8)
 
-        @pl.when(t == 8)
+        @pl.when(t == 6)
         def _():
             relay("big", 1)
             relay("big", 2)
+
+        @pl.when(t == 8)
+        def _():
             far("big", 1)
             far("big", 2)
             other("big", 1)
             other("big", 2)
 
-        @pl.when(t == 20)
+        @pl.when(t == 10)
         def _():
             spread("big", 3)
 
-        @pl.when(t == 22)
+        @pl.when(t == 12)
         def _():
             relay("big", 3)
 
-        @pl.when(t == 24)
+        @pl.when(t == 14)
         def _():
             far("big", 3)
+
+        @pl.when(t == 16)
+        def _():
             other("big", 3)
 
-        g = t // 8
-        turn = ((g + 3) // 4) * (1 + (g + 1) % 3)
-        zz = (z + step * turn + 16) % 4
-        n = zz * 8 + (sub - t % 8 + 8) % 8
+        @pl.when((t % 8 == 0) & (t < 24))
+        def _():
+            q = t // 8
+            lax.fori_loop(q + q // 2, q + 1 + (q + 1) // 2, rotate, 0)
+
+        turn = turn_of(t // 8)
+        n = slot(step * turn, 4 - t % 8 // 2, (c + t) % 2)
         col_copy(partner, n).wait_recv()
         acts_n = jnp.dot(cols[n], ub_v[...], preferred_element_type=F32).astype(BF16)
         for i in range(4):
             at = slice(i * 256, (i + 1) * 256)
-            grads_n = jnp.dot(big[n], basis_v[:, at], preferred_element_type=F32).astype(BF16)
             gradient = lax.dot_general(
-                grads_n, acts_n, (((0,), (0,)), ((), ())), preferred_element_type=F32
+                rotated[n, :, at], acts_n, (((0,), (0,)), ((), ())), preferred_element_type=F32
             )
             scaled_v[at, :] = (gradient * inv_v[at, :]).astype(BF16)
         for i in range(4):
@@ -374,6 +401,7 @@
             pltpu.VMEM((32, 128, 1024), BF16),
             pltpu.VMEM((32, 128, 256), BF16),
             pltpu.VMEM((1024, 1024), BF16),
+            pltpu.VMEM((32, 128, 1024), BF16),
             pltpu.VMEM((1024, 1024), BF16),
             pltpu.VMEM((256, 256), BF16),
             pltpu.VMEM((1024, 256), BF16),

time: 216 us -> 201 us (0.931)
  Pallas kernels: 215 us -> 200 us
    pallas_call x1, Pallas kernels: 215 us -> 200 us  [on_device(): pl.pallas_call(kernel, out_shape=jax.ShapeDtypeStruct((1, 32), F32), in_s...]
where the time goes in v2:
time: 201 us
  Pallas kernels  200 us (100%)
    pallas_call x1, Pallas kernels, on_device(): pl.pallas_call(kernel, out_shape=jax.ShapeDtypeStruct((1, 32), F32), in_s...  200 us

profile of v2, /device:TPU:1, one launch (start us, length us, event | category | flops | bytes accessed | tf_op | source)
XLA Modules:
  0.0 201.1 jit_solution(6427479359609039528)
XLA Ops:
  0.0 199.9 %influence.1 = f32[1,32]{1,0:T(1,128)} custom-call(bf16[128,8192]{1,0:T(8,128)(2,1)} %bitcast.10, bf16[128,1024]{1,0:T(8,128)(2,1)} %bitcast.13, bf16[256,256]{1,0:T(8,128)(2,1)} %bitcast.14, bf16[32,1024]{1,0:T(8,128)(2,1)} %bitcast.15, bf16[1024,256]{1,0:T(8,128)(2,1)} %bitcast.11, bf16[32,1024]{1,0:T(8,128)(2,1)} %bitcast.16, ...), custom_call_target="tpu_custom_call" | custom-call | tf_op jit(solution)/shard_map/influence/pallas_call | solution.py:394
  199.9 1.2 copy.11

commit v3 on v2

--- a/solution.py
+++ b/solution.py
@@ -50,6 +50,7 @@
     sec_ss,
     sec_rs,
     loc,
+    known,
 ):
     n_dev = 32
     n_sec = 16
@@ -80,11 +81,17 @@
 
     barrier = pltpu.get_barrier_semaphore()
 
-    def greet(o, _):
-        pl.semaphore_signal(
-            barrier, inc=1, device_id={"dp": (me + o) % n_dev}, device_id_type=MESH
-        )
-        return 0
+    def greet(dz):
+        def one(j, _):
+            pl.semaphore_signal(
+                barrier,
+                inc=1,
+                device_id={"dp": slot(dz, j // 2, (c + j) % 2)},
+                device_id_type=MESH,
+            )
+            return 0
+
+        return one
 
     def greet_sec(o, _):
         pl.semaphore_signal(
@@ -92,13 +99,16 @@
         )
         return 0
 
-    lax.fori_loop(1, n_dev, greet, 0)
+    lax.fori_loop(0, 8, greet(1), 0)
+    lax.fori_loop(0, 8, greet(-1), 0)
+    lax.fori_loop(1, 8, greet(0), 0)
     lax.fori_loop(1, n_sec, greet_sec, 0)
     rows_v[...] = jnp.zeros_like(rows_v)
     l_u.wait()
     l_l.wait()
     l_g.wait()
-    pl.semaphore_wait(barrier, n_dev - 1 + n_sec - 1)
+    pl.semaphore_wait(barrier, 23 + n_sec - 1)
+    pl.semaphore_signal(known, inc=1, device_id={"dp": slot(-1, 0, c)}, device_id_type=MESH)
 
     counts = {"small": 0, "big": 0}
     parts = {"small": (small, small_ss, small_rs), "big": (big, big_ss, big_rs)}
@@ -208,6 +218,7 @@
         return 0
 
     lax.fori_loop(0, n_dev, lay, 0)
+    pl.semaphore_wait(known, 1)
     other("big", 0)
 
     ones = jnp.ones((8, 128), F32)
@@ -234,8 +245,11 @@
         def _():
             spread("big", 1)
             spread("big", 2)
+            col_sends((2,), 0, 8)
+
+        @pl.when(t == 3 + 9 * (sec % 4 // 2))
+        def _():
             col_sends((1, -1), 4, 8)
-            col_sends((2,), 0, 8)
 
         @pl.when(t == 6)
         def _():
@@ -270,8 +284,18 @@
             q = t // 8
             lax.fori_loop(q + q // 2, q + 1 + (q + 1) // 2, rotate, 0)
 
-        turn = turn_of(t // 8)
-        n = slot(step * turn, 4 - t % 8 // 2, (c + t) % 2)
+        @pl.when(t == 26)
+        def _():
+            for kind in ("small", "big"):
+                for i in range(counts[kind]):
+                    copy_of(kind, i, me, partner).wait_send()
+
+        u = t // 4
+        half = (u + 3) // 8 + ((u + 7) // 8) * ((9 - u) // 8)
+        r = (u + 2) % 4
+        turn = ((u + 6) // 8) * ((1 - r // 2) * (3 - 2 * r) + 2 * (r // 2))
+        j = half * 4 + t % 4
+        n = slot(step * turn, 4 - j // 2, (c + j) % 2)
         col_copy(partner, n).wait_recv()
         acts_n = jnp.dot(cols[n], ub_v[...], preferred_element_type=F32).astype(BF16)
         for i in range(4):
@@ -306,10 +330,6 @@
 
     if counts != {"small": 31, "big": 31}:
         raise ValueError(str(counts))
-
-    for kind in ("small", "big"):
-        for i in range(counts[kind]):
-            copy_of(kind, i, me, partner).wait_send()
 
     def col_left(o, _):
         col_copy((me + o) % n_dev, me).wait_send()
@@ -425,6 +445,7 @@
             sems((16,)),
             sems((16,)),
             sems((6,)),
+            pltpu.SemaphoreType.REGULAR,
         ],
         compiler_params=pltpu.CompilerParams(
             collective_id=0, has_side_effects=True, vmem_limit_bytes=56 * 2**20

time: 201 us -> 221 us (1.100)
  Pallas kernels: 200 us -> 220 us
    pallas_call x1, Pallas kernels: 200 us -> 220 us  [on_device(): pl.pallas_call(kernel, out_shape=jax.ShapeDtypeStruct((1, 32), F32), in_s...]
where the time goes in v3:
time: 221 us
  Pallas kernels  220 us (100%)
    pallas_call x1, Pallas kernels, on_device(): pl.pallas_call(kernel, out_shape=jax.ShapeDtypeStruct((1, 32), F32), in_s...  220 us

profile of v3, /device:TPU:1, one launch (start us, length us, event | category | flops | bytes accessed | tf_op | source)
XLA Modules:
  0.0 221.3 jit_solution(3351421938317121794)
XLA Ops:
  0.0 220.1 %influence.1 = f32[1,32]{1,0:T(1,128)} custom-call(bf16[128,8192]{1,0:T(8,128)(2,1)} %bitcast.10, bf16[128,1024]{1,0:T(8,128)(2,1)} %bitcast.13, bf16[256,256]{1,0:T(8,128)(2,1)} %bitcast.14, bf16[32,1024]{1,0:T(8,128)(2,1)} %bitcast.15, bf16[1024,256]{1,0:T(8,128)(2,1)} %bitcast.11, bf16[32,1024]{1,0:T(8,128)(2,1)} %bitcast.16, ...), custom_call_target="tpu_custom_call" | custom-call | tf_op jit(solution)/shard_map/influence/pallas_call | solution.py:414
  220.1 1.2 copy.11

commit v4 on v2

--- a/solution.py
+++ b/solution.py
@@ -234,8 +234,11 @@
         def _():
             spread("big", 1)
             spread("big", 2)
+            col_sends((2,), 0, 8)
+
+        @pl.when(t == 3 + 9 * (sec % 4 // 2))
+        def _():
             col_sends((1, -1), 4, 8)
-            col_sends((2,), 0, 8)
 
         @pl.when(t == 6)
         def _():
@@ -270,8 +273,18 @@
             q = t // 8
             lax.fori_loop(q + q // 2, q + 1 + (q + 1) // 2, rotate, 0)
 
-        turn = turn_of(t // 8)
-        n = slot(step * turn, 4 - t % 8 // 2, (c + t) % 2)
+        @pl.when(t == 26)
+        def _():
+            for kind in ("small", "big"):
+                for i in range(counts[kind]):
+                    copy_of(kind, i, me, partner).wait_send()
+
+        u = t // 4
+        half = (u + 3) // 8 + ((u + 7) // 8) * ((9 - u) // 8)
+        r = (u + 2) % 4
+        turn = ((u + 6) // 8) * ((1 - r // 2) * (3 - 2 * r) + 2 * (r // 2))
+        j = half * 4 + t % 4
+        n = slot(step * turn, 4 - j // 2, (c + j) % 2)
         col_copy(partner, n).wait_recv()
         acts_n = jnp.dot(cols[n], ub_v[...], preferred_element_type=F32).astype(BF16)
         for i in range(4):
@@ -306,10 +319,6 @@
 
     if counts != {"small": 31, "big": 31}:
         raise ValueError(str(counts))
-
-    for kind in ("small", "big"):
-        for i in range(counts[kind]):
-            copy_of(kind, i, me, partner).wait_send()
 
     def col_left(o, _):
         col_copy((me + o) % n_dev, me).wait_send()

time: 201 us -> 216 us (1.075)
  Pallas kernels: 200 us -> 214 us
    pallas_call x1, Pallas kernels: 200 us -> 214 us  [on_device(): pl.pallas_call(kernel, out_shape=jax.ShapeDtypeStruct((1, 32), F32), in_s...]
where the time goes in v4:
time: 216 us
  Pallas kernels  214 us (99%)
    pallas_call x1, Pallas kernels, on_device(): pl.pallas_call(kernel, out_shape=jax.ShapeDtypeStruct((1, 32), F32), in_s...  214 us

profile of v4, /device:TPU:1, one launch (start us, length us, event | category | flops | bytes accessed | tf_op | source)
XLA Modules:
  0.0 215.6 jit_solution(4213986780355474701)
XLA Ops:
  0.0 214.4 %influence.1 = f32[1,32]{1,0:T(1,128)} custom-call(bf16[128,8192]{1,0:T(8,128)(2,1)} %bitcast.10, bf16[128,1024]{1,0:T(8,128)(2,1)} %bitcast.13, bf16[256,256]{1,0:T(8,128)(2,1)} %bitcast.14, bf16[32,1024]{1,0:T(8,128)(2,1)} %bitcast.15, bf16[1024,256]{1,0:T(8,128)(2,1)} %bitcast.11, bf16[32,1024]{1,0:T(8,128)(2,1)} %bitcast.16, ...), custom_call_target="tpu_custom_call" | custom-call | tf_op jit(solution)/shard_map/influence/pallas_call | solution.py:403
  214.4 1.2 copy.11
